TPU v7x, 32 devices: a whole 2x2x4 slice. The times are simulated.
32 devices in a mesh: row: 4 (over y, x), col: 4 (over z), depth: 2 (over core).
Axes of the slice: x: 2, y: 2, z: 4, core: 2. Of those that a mesh axis runs over, the one named last changes fastest.
Arguments:
- matrix_panel: bfloat16 [12288, 65536], P('row', 'col'), may hold values from -0.1484375 to 0.1484375
- start_block: bfloat16 [12288, 64], P('row', 'depth'), may hold values from -6 to 6
- stored_basis: float32 [12288, 1024], P('row'), may hold values from -2.2 to 2.2
Outputs:
- new_block: float32 [12288, 64], P('row', 'depth')
- coefficients: float32 [1024, 64], P(None, 'depth')
- triangle: float32 [64, 64], replicated
All inputs are finite; a program needn't handle non-finite values.
Results may differ from a plain program's by a relative error of at most 0.0023.
Values may be sent and summed in bfloat16 or wider, within the bound.
A program may use at most 256 MiB of HBM per device.

v0:
```python
import jax
import jax.numpy as jnp
from jax import lax
from jax.sharding import PartitionSpec as P

HIGHEST = lax.Precision.HIGHEST


def contract_rows(left_side, right_side, mode):
    return lax.dot_general(
        left_side,
        right_side,
        (((0,), (0,)), ((), ())),
        precision=mode,
        preferred_element_type=jnp.float32,
    )


def factor_gram(gram_matrix):
    lower_factor = jnp.linalg.cholesky(gram_matrix)
    identity = jnp.eye(gram_matrix.shape[0], dtype=jnp.float32)
    inverse = jax.scipy.linalg.solve_triangular(lower_factor, identity, lower=True)
    return (lower_factor, inverse)


def orthonormal_pass(stored_basis, block_cols, reduce_sum, row_total):
    projection = reduce_sum(contract_rows(stored_basis, block_cols, HIGHEST)) / row_total
    remainder = block_cols - jnp.dot(
        stored_basis, projection, precision=HIGHEST, preferred_element_type=jnp.float32
    )
    gram_matrix = reduce_sum(contract_rows(remainder, remainder, HIGHEST)) / row_total
    lower_factor, inverse = factor_gram(gram_matrix)
    normed = jnp.dot(remainder, inverse.T, precision=HIGHEST, preferred_element_type=jnp.float32)
    return (projection, lower_factor, normed)


def per_device(matrix_panel, start_block, stored_basis):
    row_total = stored_basis.shape[0] * lax.axis_size("row")
    half_cols = start_block.shape[1]
    depth_index = lax.axis_index("depth")
    whole_start = lax.all_gather(start_block, "depth", axis=1, tiled=True)
    half_rows = matrix_panel.shape[0] // 2
    panel_rows = lax.dynamic_slice_in_dim(matrix_panel, depth_index * half_rows, half_rows, 0)
    start_rows = lax.dynamic_slice_in_dim(whole_start, depth_index * half_rows, half_rows, 0)
    basis_rows = lax.dynamic_slice_in_dim(stored_basis, depth_index * half_rows, half_rows, 0)
    mixed_cols = lax.psum(contract_rows(panel_rows, start_rows, None), ("row", "depth")).astype(
        jnp.bfloat16
    )
    image_block = lax.psum(
        jnp.dot(panel_rows, mixed_cols, preferred_element_type=jnp.float32), "col"
    )

    def sum_layers(value):
        return lax.psum(value, ("row", "depth"))

    proj_first, lower_first, normed_first = orthonormal_pass(
        basis_rows, image_block, sum_layers, row_total
    )
    proj_second, lower_second, normed_second = orthonormal_pass(
        basis_rows, normed_first, sum_layers, row_total
    )
    new_block = lax.all_to_all(normed_second, "depth", split_axis=1, concat_axis=0, tiled=True)
    coef_whole = proj_first + jnp.dot(
        proj_second, lower_first.T, precision=HIGHEST, preferred_element_type=jnp.float32
    )
    coefficients = lax.dynamic_slice_in_dim(coef_whole, depth_index * half_cols, half_cols, 1)
    triangle = jnp.dot(
        lower_second.T, lower_first.T, precision=HIGHEST, preferred_element_type=jnp.float32
    )
    return (new_block, coefficients, triangle)


def solution(mesh):
    placed = (P("row", "col"), P("row", "depth"), P("row", None))
    return jax.shard_map(
        per_device,
        mesh=mesh,
        in_specs=placed,
        out_specs=(P("row", "depth"), P(None, "depth"), P()),
        check_vma=False,
    )
```

profile of v0, /device:TPU:0, one launch (start us, length us, event | category | flops | bytes accessed | tf_op | source)
XLA Modules:
  0.0 405.6 jit_solution(3928022254567349980)
XLA Ops:
  7.2 0.0 all-reduce.5.cloned.1.call-start
  7.2 2.4 all_gather.3
  9.6 20.5 %fusion.2 = f32[16384,64]{0,1:T(8,128)} fusion(bf16[3072,16384]{1,0:T(8,128)(2,1)} %param.6, s32[]{:T(128)S(6)} %select_n.11, bf16[3072,64]{0,1:T(8,128)(2,1)S(1)} %all_gather.3), kind=kOutput, calls=%fused_computation.2 | convolution fusion | flops 3221225472 | bytes 54723584 | tf_op jit(solution)/shard_map/dot_general | solution.py:10
  30.1 89.5 %all-reduce.10 = bf16[16384,64]{0,1:T(8,128)(2,1)S(1)} all-reduce(f32[16384,64]{0,1:T(8,128)} %fusion.2), channel_id=1, replica_groups=mesh['row'=4,'col'=4,'depth'=2] {'row','depth'}, use_global_device_ids=true, to_apply=%region_0.0 | all-reduce | flops 1048576 | bytes 6291456 | tf_op jit(solution)/shard_map/psum | solution.py:46
  119.6 22.6 %fusion = f32[1536,64]{0,1:T(8,128)} fusion(bf16[3072,16384]{1,0:T(8,128)(2,1)} %param.6, s32[]{:T(128)S(6)} %select_n.11, bf16[16384,64]{0,1:T(8,128)(2,1)S(1)} %all-reduce.10), kind=kOutput, calls=%fused_computation | convolution fusion | flops 3221225472 | bytes 52822020 | tf_op jit(solution)/shard_map/dot_general | solution.py:50
  142.2 0.0 all-reduce.5.cloned.1.call-update
  142.2 0.0 all-reduce.7.cloned.1.call-start
  142.3 36.9 %all-reduce.5.cloned.1.call-done = f32[1536,64]{0,1:T(8,128)} async-done(((f32[1536,64]{0,1:T(8,128)}), f32[1536,64]{0,1:T(8,128)}) %all-reduce.5.cloned.1.call-update) | async-done | bytes 393232 | tf_op jit(solution)/shard_map/psum | solution.py:49
  179.2 7.6 %fusion.10 = f32[1024,64]{0,1:T(8,128)} fusion(f32[1536,64]{0,1:T(8,128)} %all-reduce.5.cloned.1.call-done, f32[3072,1024]{1,0:T(8,128)} %param.8, s32[]{:T(128)S(6)} %select_n.11), kind=kOutput, calls=%fused_computation.10 | convolution fusion | flops 1207959552 | bytes 6946820 | tf_op jit(solution)/shard_map/dot_general | solution.py:10
  186.8 0.0 all-reduce.7.cloned.1.call-update
  186.8 0.2 all-reduce.9.cloned.1.call-start
  187.0 53.1 %all-reduce.7.cloned.1.call-done = f32[1024,64]{0,1:T(8,128)} async-done(((f32[1024,64]{0,1:T(8,128)}), f32[1024,64]{0,1:T(8,128)}) %all-reduce.7.cloned.1.call-update) | async-done | bytes 262160 | tf_op jit(solution)/shard_map/psum | solution.py:54
  240.1 0.0 copy-start
  240.1 9.1 %fusion.12 = f32[1536,64]{0,1:T(8,128)S(1)} fusion(f32[1536,64]{0,1:T(8,128)} %all-reduce.5.cloned.1.call-done, f32[3072,1024]{1,0:T(8,128)} %param.8, s32[]{:T(128)S(6)} %select_n.11, f32[1024,64]{0,1:T(8,128)} %all-reduce.7.cloned.1.call-done), kind=kOutput, calls=%fused_computation.12 | convolution fusion | flops 1208123392 | bytes 7340036 | tf_op jit(solution)/shard_map/dot_general | solution.py:28
  249.2 0.5 fusion.56
  249.6 22.4 %psum.45 = f32[64,64]{0,1:T(8,128)S(1)} all-reduce(f32[64,64]{0,1:T(8,128)S(1)} %fusion.56), channel_id=1, replica_groups=mesh['row'=4,'col'=4,'depth'=2] {'row','depth'}, use_global_device_ids=true, to_apply=%region_3.0 | all-reduce | flops 4096 | bytes 32768 | tf_op jit(solution)/shard_map/psum | solution.py:54
  272.0 0.1 copy.12
  272.1 5.8 %cholesky.44 = f32[64,64]{1,0:T(8,128)S(1)} custom-call(f32[64,64]{1,0:T(8,128)S(1)} %fusion.32), custom_call_target="Cholesky" | custom-call | tf_op jit(solution)/shard_map/jit(cholesky)/cholesky | solution.py:20
  278.0 0.6 compare_reduce_fusion.1
  278.6 0.7 select_bitcast_fusion.1
  279.3 4.9 %custom-call.6 = f32[1,64,64]{1,2,0:T(8,128)S(1)} custom-call(f32[1,64,64]{2,1,0:T(8,128)S(1)} %select_bitcast_fusion.1), custom_call_target="InvertDiagBlocksLowerTriangular" | custom-call | tf_op jit(solution)/shard_map/jit(_solve_triangular)/triangular_solve | solution.py:22
  284.2 0.3 fusion.27
  284.4 0.5 fusion.57
  284.9 7.6 %fusion.6 = f32[1024,64]{0,1:T(8,128)} fusion(f32[1536,64]{0,1:T(8,128)S(1)} %fusion.57, f32[3072,1024]{1,0:T(8,128)} %param.8, s32[]{:T(128)S(6)} %select_n.11), kind=kOutput, calls=%fused_computation.6 | convolution fusion | flops 1207959552 | bytes 6946820 | tf_op jit(solution)/shard_map/dot_general | solution.py:10
  292.5 0.0 all-reduce.9.cloned.1.call-update
  292.5 0.0 copy-done
  292.5 53.0 %all-reduce.9.cloned.1.call-done = f32[1024,64]{0,1:T(8,128)} async-done(((f32[1024,64]{0,1:T(8,128)}), f32[1024,64]{0,1:T(8,128)}) %all-reduce.9.cloned.1.call-update) | async-done | bytes 262160 | tf_op jit(solution)/shard_map/psum | solution.py:54
  345.5 8.1 %fusion.15 = f32[1536,64]{0,1:T(8,128)S(1)} fusion(f32[1536,64]{0,1:T(8,128)S(1)} %fusion.57, f32[3072,1024]{1,0:T(8,128)} %param.8, s32[]{:T(128)S(6)} %select_n.11, f32[1024,64]{0,1:T(8,128)} %all-reduce.9.cloned.1.call-done), kind=kOutput, calls=%fused_computation.13 | convolution fusion | flops 1208123392 | bytes 7340036 | tf_op jit(solution)/shard_map/dot_general | solution.py:28
  353.7 0.5 fusion.58
  354.1 22.4 %psum.47 = f32[64,64]{0,1:T(8,128)S(1)} all-reduce(f32[64,64]{0,1:T(8,128)S(1)} %fusion.58), channel_id=1, replica_groups=mesh['row'=4,'col'=4,'depth'=2] {'row','depth'}, use_global_device_ids=true, to_apply=%region_7.10 | all-reduce | flops 4096 | bytes 32768 | tf_op jit(solution)/shard_map/psum | solution.py:54
  376.5 0.1 copy.14
  376.6 5.8 %cholesky.55 = f32[64,64]{1,0:T(8,128)S(1)} custom-call(f32[64,64]{1,0:T(8,128)S(1)} %fusion.30), custom_call_target="Cholesky" | custom-call | tf_op jit(solution)/shard_map/jit(cholesky)/cholesky | solution.py:20
  382.5 0.6 compare_reduce_fusion
  383.1 2.1 fusion.34
  385.3 0.7 select_bitcast_fusion
  385.9 4.9 %custom-call.7 = f32[1,64,64]{1,2,0:T(8,128)S(1)} custom-call(f32[1,64,64]{2,1,0:T(8,128)S(1)} %select_bitcast_fusion), custom_call_target="InvertDiagBlocksLowerTriangular" | custom-call | tf_op jit(solution)/shard_map/jit(_solve_triangular)/triangular_solve | solution.py:22
  390.8 0.3 fusion.25
  391.1 0.5 fusion.59
  391.6 4.0 all_to_all.19
  395.6 0.8 copy.18
  396.4 2.0 fusion.19
  398.4 0.7 dynamic-slice_add_fusion
  (7 shorter events, 0.1 us)
Async XLA Ops:
  7.2 172.0 %all-reduce.5.cloned.1.call-start = ((), (), s32[]{:S(2)}) async-start(), calls=%async_computation.1 | async-start | bytes 786432 | tf_op jit(solution)/shard_map/psum | solution.py:49
  142.2 97.8 %all-reduce.7.cloned.1.call-start = ((), (), s32[]{:S(2)}) async-start(), calls=%async_computation.2 | async-start | bytes 524288 | tf_op jit(solution)/shard_map/psum | solution.py:54
  186.8 158.8 %all-reduce.9.cloned.1.call-start = ((), (), s32[]{:S(2)}) async-start(), calls=%async_computation.3 | async-start | bytes 524288 | tf_op jit(solution)/shard_map/psum | solution.py:54
  240.1 52.4 %copy-start = (f32[1024,64]{0,1:T(8,128)S(1)}, f32[1024,64]{0,1:T(8,128)}, u32[]{:S(2)}) copy-start(f32[1024,64]{0,1:T(8,128)} %all-reduce.7.cloned.1.call-done) | copy-start | bytes 786436
Sparse Core Ops, SparseCore 0:
  142.3 36.8 all-reduce.4
  186.9 53.1 all-reduce.6
  292.6 52.8 all-reduce.8
where the time goes:
time: 406 us
  waiting for transfers between devices  143 us (35%)
  blocking collectives  141 us (35%)
  matrix products  82 us (20%)
  other arithmetic  24.9 us (6%)
  between operations  13.9 us (3%)
    psum x2, waiting for transfers between devices, sum_layers(): return lax.psum(value, ('row', 'depth'))  106 us
    psum x1, blocking collectives, per_device(): lax.psum(contract_rows(panel_rows, start_rows, None), ('row', 'depth'))  89.5 us
    psum x2, blocking collectives, sum_layers(): return lax.psum(value, ('row', 'depth'))  44.7 us
    psum x1, waiting for transfers between devices, per_device(): lax.psum(jnp.dot(panel_rows, mixed_cols, preferred_element_type=jnp.float...  36.9 us
    dot_general x5, matrix products, contract_rows(): lax.dot_general(left_side, right_side, (((0,), (0,)), ((), ())), precisio...  36.5 us
    dot_general x1, matrix products, per_device(): jnp.dot(panel_rows, mixed_cols, preferred_element_type=jnp.float32)  22.6 us
    dot_general x2, matrix products, orthonormal_pass(): jnp.dot(stored_basis, projection, precision=HIGHEST, preferred_element_ty...  17.2 us
    another operation x6, other arithmetic, factor_gram(): lower_factor = jnp.linalg.cholesky(gram_matrix)  13 us
  transfers between devices with their start and end apart: 3, of which 3 were waited for; matrix products, arithmetic and copies ran while one was open for 0% of the time, Pallas kernels for 0%

commit v1 on v0

--- a/solution.py
+++ b/solution.py
@@ -2,6 +2,7 @@
 import jax.numpy as jnp
 from jax import lax
 from jax.sharding import PartitionSpec as P
+from jax.lax import all_gather
 
 HIGHEST = lax.Precision.HIGHEST
 
@@ -43,9 +44,9 @@
     panel_rows = lax.dynamic_slice_in_dim(matrix_panel, depth_index * half_rows, half_rows, 0)
     start_rows = lax.dynamic_slice_in_dim(whole_start, depth_index * half_rows, half_rows, 0)
     basis_rows = lax.dynamic_slice_in_dim(stored_basis, depth_index * half_rows, half_rows, 0)
-    mixed_cols = lax.psum(contract_rows(panel_rows, start_rows, None), ("row", "depth")).astype(
-        jnp.bfloat16
-    )
+    mixed_cols = jnp.sum(
+        all_gather(contract_rows(panel_rows, start_rows, None), ("row", "depth")), axis=0
+    ).astype(jnp.bfloat16)
     image_block = lax.psum(
         jnp.dot(panel_rows, mixed_cols, preferred_element_type=jnp.float32), "col"
     )

time: 406 us -> 521 us (1.28)
  waiting for transfers between devices: 143 us -> 307 us
  blocking collectives: 141 us -> 51.4 us
  local copies, waits for them, and re-layouts: 0.93 us -> 29.1 us
  other arithmetic: 24.9 us -> 36.9 us
    all_gather x0 -> x1, waiting for transfers between devices: none -> 164 us  [per_device(): all_gather(contract_rows(panel_rows, start_rows, None), ('row', 'depth'))]
    psum x1 -> x0, blocking collectives: 89.5 us -> none  [per_device(): lax.psum(contract_rows(panel_rows, start_rows, None), ('row', 'depth'))]
    unnamed x2 -> x3, local copies, waits for them, and re-layouts: 0.01 us -> 28.2 us
    reduce_sum x0 -> x1, other arithmetic: none -> 12 us  [per_device(): jnp.sum(all_gather(contract_rows(panel_rows, start_rows, None), ('row', '...]
  transfers between devices with their start and end apart: 3 -> 4, of which waited for: 3 -> 4; matrix products, arithmetic and copies ran while one was open for 0% -> 0% of each run, Pallas kernels for 0% -> 0%
where the time goes in v1:
time: 521 us
  waiting for transfers between devices  307 us (59%)
  matrix products  82.7 us (16%)
  blocking collectives  51.4 us (10%)
  other arithmetic  36.9 us (7%)
  local copies, waits for them, and re-layouts  29.1 us (6%)
  between operations  13.9 us (3%)
    all_gather x1, waiting for transfers between devices, per_device(): all_gather(contract_rows(panel_rows, start_rows, None), ('row', 'depth'))  164 us
    psum x2, waiting for transfers between devices, sum_layers(): return lax.psum(value, ('row', 'depth'))  106 us
    psum x2, blocking collectives, sum_layers(): return lax.psum(value, ('row', 'depth'))  44.9 us
    psum x1, waiting for transfers between devices, per_device(): lax.psum(jnp.dot(panel_rows, mixed_cols, preferred_element_type=jnp.float...  37 us
    dot_general x5, matrix products, contract_rows(): lax.dot_general(left_side, right_side, (((0,), (0,)), ((), ())), precisio...  36.7 us
    unnamed x3, local copies, waits for them, and re-layouts  28.2 us
    dot_general x1, matrix products, per_device(): jnp.dot(panel_rows, mixed_cols, preferred_element_type=jnp.float32)  23.2 us
    dot_general x2, matrix products, orthonormal_pass(): jnp.dot(stored_basis, projection, precision=HIGHEST, preferred_element_ty...  17.2 us
  transfers between devices with their start and end apart: 4, of which 4 were waited for; matrix products, arithmetic and copies ran while one was open for 0% of the time, Pallas kernels for 0%

profile of v1, /device:TPU:0, one launch (start us, length us, event | category | flops | bytes accessed | tf_op | source)
XLA Modules:
  0.0 521.1 jit_solution(12249975972337129338)
XLA Ops:
  7.2 0.0 all-gather.3.cloned.1.call-start
  7.2 2.4 all_gather.9
  9.6 20.6 %fusion.2 = f32[16384,64]{0,1:T(8,128)} fusion(bf16[3072,16384]{1,0:T(8,128)(2,1)} %param.6, s32[]{:T(128)S(6)} %select_n.11, bf16[3072,64]{0,1:T(8,128)(2,1)S(1)} %all_gather.9), kind=kOutput, calls=%fused_computation.2 | convolution fusion | flops 3221225472 | bytes 54723584 | tf_op jit(solution)/shard_map/dot_general | solution.py:11
  30.2 0.0 all-gather.3.cloned.1.call-update
  30.3 0.0 all-reduce.4.cloned.1.call-start
  30.3 163.5 %all-gather.3.cloned.1.call-done = f32[131072,64]{0,1:T(8,128)} async-done(((f32[16384,64]{0,1:T(8,128)}), f32[131072,64]{0,1:T(8,128)}) %all-gather.3.cloned.1.call-update) | async-done | bytes 33554448 | tf_op jit(solution)/shard_map/all_gather | solution.py:48
  193.8 28.2 %copy.19 = f32[8,8,8,16384]{3,2,1,0:T(8,128)S(1)} copy(f32[8,8,8,16384]{3,1,2,0:T(8,128)} %bitcast.38) | data formatting | bytes 67108864
  222.0 12.0 %bitcast_reduce_fusion = bf16[16384,64]{0,1:T(8,128)(2,1)} fusion(f32[8,8,8,16384]{3,2,1,0:T(8,128)S(1)} %copy.19), kind=kLoop, calls=%fused_computation.4 | loop fusion | flops 7340032 | bytes 35651584 | tf_op jit(solution)/shard_map/reduce_sum | solution.py:47
  234.0 23.2 %fusion = f32[1536,64]{0,1:T(8,128)} fusion(bf16[3072,16384]{1,0:T(8,128)(2,1)} %param.6, s32[]{:T(128)S(6)} %select_n.11, bf16[16384,64]{0,1:T(8,128)(2,1)} %bitcast_reduce_fusion), kind=kOutput, calls=%fused_computation | convolution fusion | flops 3221225472 | bytes 52822020 | tf_op jit(solution)/shard_map/dot_general | solution.py:51
  257.2 0.0 all-reduce.4.cloned.1.call-update
  257.3 0.2 all-reduce.6.cloned.1.call-start
  257.5 37.0 %all-reduce.4.cloned.1.call-done = f32[1536,64]{0,1:T(8,128)} async-done(((f32[1536,64]{0,1:T(8,128)}), f32[1536,64]{0,1:T(8,128)}) %all-reduce.4.cloned.1.call-update) | async-done | bytes 393232 | tf_op jit(solution)/shard_map/psum | solution.py:50
  294.5 7.6 %fusion.10 = f32[1024,64]{0,1:T(8,128)} fusion(f32[1536,64]{0,1:T(8,128)} %all-reduce.4.cloned.1.call-done, f32[3072,1024]{1,0:T(8,128)} %param.8, s32[]{:T(128)S(6)} %select_n.11), kind=kOutput, calls=%fused_computation.11 | convolution fusion | flops 1207959552 | bytes 6946820 | tf_op jit(solution)/shard_map/dot_general | solution.py:11
  302.1 0.0 all-reduce.6.cloned.1.call-update
  302.1 0.0 all-reduce.8.cloned.1.call-start
  302.1 53.2 %all-reduce.6.cloned.1.call-done = f32[1024,64]{0,1:T(8,128)} async-done(((f32[1024,64]{0,1:T(8,128)}), f32[1024,64]{0,1:T(8,128)}) %all-reduce.6.cloned.1.call-update) | async-done | bytes 262160 | tf_op jit(solution)/shard_map/psum | solution.py:55
  355.4 0.0 copy-start
  355.4 9.1 %fusion.12 = f32[1536,64]{0,1:T(8,128)S(1)} fusion(f32[1536,64]{0,1:T(8,128)} %all-reduce.4.cloned.1.call-done, f32[3072,1024]{1,0:T(8,128)} %param.8, s32[]{:T(128)S(6)} %select_n.11, f32[1024,64]{0,1:T(8,128)} %all-reduce.6.cloned.1.call-done), kind=kOutput, calls=%fused_computation.13 | convolution fusion | flops 1208123392 | bytes 7340036 | tf_op jit(solution)/shard_map/dot_general | solution.py:29
  364.5 0.5 fusion.56
  364.9 22.6 %psum.37 = f32[64,64]{0,1:T(8,128)S(1)} all-reduce(f32[64,64]{0,1:T(8,128)S(1)} %fusion.56), channel_id=1, replica_groups=mesh['row'=4,'col'=4,'depth'=2] {'row','depth'}, use_global_device_ids=true, to_apply=%region_3.0 | all-reduce | flops 4096 | bytes 32768 | tf_op jit(solution)/shard_map/psum | solution.py:55
  387.5 0.1 copy.12
  387.6 5.8 %cholesky.44 = f32[64,64]{1,0:T(8,128)S(1)} custom-call(f32[64,64]{1,0:T(8,128)S(1)} %fusion.32), custom_call_target="Cholesky" | custom-call | tf_op jit(solution)/shard_map/jit(cholesky)/cholesky | solution.py:21
  393.5 0.6 compare_reduce_fusion.1
  394.1 0.7 select_bitcast_fusion.1
  394.8 4.9 custom-call.6
  399.7 0.3 fusion.27
  400.0 0.5 fusion.57
  400.4 7.6 %fusion.6 = f32[1024,64]{0,1:T(8,128)} fusion(f32[1536,64]{0,1:T(8,128)S(1)} %fusion.57, f32[3072,1024]{1,0:T(8,128)} %param.8, s32[]{:T(128)S(6)} %select_n.11), kind=kOutput, calls=%fused_computation.7 | convolution fusion | flops 1207959552 | bytes 6946820 | tf_op jit(solution)/shard_map/dot_general | solution.py:11
  408.0 0.0 all-reduce.8.cloned.1.call-update
  408.0 0.0 copy-done
  408.1 53.0 %all-reduce.8.cloned.1.call-done = f32[1024,64]{0,1:T(8,128)} async-done(((f32[1024,64]{0,1:T(8,128)}), f32[1024,64]{0,1:T(8,128)}) %all-reduce.8.cloned.1.call-update) | async-done | bytes 262160 | tf_op jit(solution)/shard_map/psum | solution.py:55
  461.1 8.1 %fusion.15 = f32[1536,64]{0,1:T(8,128)S(1)} fusion(f32[1536,64]{0,1:T(8,128)S(1)} %fusion.57, f32[3072,1024]{1,0:T(8,128)} %param.8, s32[]{:T(128)S(6)} %select_n.11, f32[1024,64]{0,1:T(8,128)} %all-reduce.8.cloned.1.call-done), kind=kOutput, calls=%fused_computation.14 | convolution fusion | flops 1208123392 | bytes 7340036 | tf_op jit(solution)/shard_map/dot_general | solution.py:29
  469.2 0.5 fusion.58
  469.7 22.4 %psum.39 = f32[64,64]{0,1:T(8,128)S(1)} all-reduce(f32[64,64]{0,1:T(8,128)S(1)} %fusion.58), channel_id=1, replica_groups=mesh['row'=4,'col'=4,'depth'=2] {'row','depth'}, use_global_device_ids=true, to_apply=%region_7.10 | all-reduce | flops 4096 | bytes 32768 | tf_op jit(solution)/shard_map/psum | solution.py:55
  492.0 0.1 copy.14
  492.1 5.8 %cholesky.55 = f32[64,64]{1,0:T(8,128)S(1)} custom-call(f32[64,64]{1,0:T(8,128)S(1)} %fusion.30), custom_call_target="Cholesky" | custom-call | tf_op jit(solution)/shard_map/jit(cholesky)/cholesky | solution.py:21
  498.0 0.6 compare_reduce_fusion
  498.6 2.1 fusion.34
  500.8 0.7 select_bitcast_fusion
  501.4 4.9 custom-call.7
  506.3 0.3 fusion.25
  506.6 0.5 fusion.59
  507.1 4.0 all_to_all.19
  511.1 0.8 copy.18
  511.9 2.0 fusion.19
  513.9 0.7 dynamic-slice_add_fusion
  (7 shorter events, 0.1 us)
Async XLA Ops:
  7.2 186.7 %all-gather.3.cloned.1.call-start = ((), (), s32[]{:S(2)}) async-start(), calls=%async_computation.4 | async-start | bytes 37748736 | tf_op jit(solution)/shard_map/all_gather | solution.py:48
  30.3 264.2 %all-reduce.4.cloned.1.call-start = ((), (), s32[]{:S(2)}) async-start(), calls=%async_computation.1 | async-start | bytes 786432 | tf_op jit(solution)/shard_map/psum | solution.py:50
  257.3 98.1 %all-reduce.6.cloned.1.call-start = ((), (), s32[]{:S(2)}) async-start(), calls=%async_computation.2 | async-start | bytes 524288 | tf_op jit(solution)/shard_map/psum | solution.py:55
  302.1 159.0 %all-reduce.8.cloned.1.call-start = ((), (), s32[]{:S(2)}) async-start(), calls=%async_computation.3 | async-start | bytes 524288 | tf_op jit(solution)/shard_map/psum | solution.py:55
  355.4 52.7 %copy-start = (f32[1024,64]{0,1:T(8,128)S(1)}, f32[1024,64]{0,1:T(8,128)}, u32[]{:S(2)}) copy-start(f32[1024,64]{0,1:T(8,128)} %all-reduce.6.cloned.1.call-done) | copy-start | bytes 786436
Sparse Core Ops, SparseCore 0:
  30.4 163.4 all-gather.2
  257.4 37.0 all-reduce.3
  302.2 53.1 all-reduce.5
  408.1 52.8 all-reduce.7
